TPU v7x, 32 devices: a whole 2x2x4 slice. The times are simulated.
32 devices in a mesh: dp: 4 (over z), section: 2 (over x), mp: 4 (over y, core).
Axes of the slice: x: 2, y: 2, z: 4, core: 2. Of those that a mesh axis runs over, the one named last changes fastest.
Arguments:
- source_rows: bfloat16 [1024, 1024], P('dp', 'mp'), may hold values from -6 to 6
- value_weight: bfloat16 [2, 1024, 1024], P('section', None, 'mp'), may hold values from -0.1875 to 0.1875
- gate_weight: bfloat16 [2, 1024, 1024], P('section', None, 'mp'), may hold values from -0.1875 to 0.1875
- kernel_weight: bfloat16 [2, 1024, 496], P('section', None, 'mp'), may hold values from -0.1875 to 0.1875
- segment_ids: int32 [8, 128], P('dp'), may hold values from 0 to 3, never falling along the last dimension, each value on 1 to 64 neighbouring positions
- out_grad: bfloat16 [1024, 1024], P('dp', 'mp'), may hold values from -6 to 6
Outputs:
- value_grad: float32 [2, 1024, 1024], P('section', 'dp', 'mp')
- gate_grad: float32 [2, 1024, 1024], P('section', 'dp', 'mp')
- kernel_grad: float32 [2, 1024, 496], P('section', 'dp', 'mp')
Inputs may be any that keep to these rules, and one draw needn't show every extreme that they name: `segment_ids`: in each microbatch row of 128 positions the sentence numbers never fall and every number from 0 up to the largest appears; a sentence covers 1 to 64 positions, and in every microbatch exactly one sentence covers 64 positions.
All inputs are finite; a program needn't handle non-finite values.
Results may differ from a plain program's by a relative error of at most 0.015.
Values may be sent and summed in bfloat16 or wider, within the bound.
A program may use at most 64 MiB of HBM per device.

v0:
```python
import jax
import jax.numpy as jnp
from jax import lax
from jax.sharding import PartitionSpec as P

KERNEL = 31


def from_behind(value, axis, steps):
    count = lax.axis_size(axis)
    initial, last = (max(0, -steps), min(count, count - steps))
    return lax.ppermute(value, axis, [(source, source + steps) for source in range(initial, last)])


def make_table(segments):
    row_count = segments.shape[0]
    positions = jnp.arange(row_count, dtype=jnp.int32)
    offsets = positions[None, :] - positions[:, None] + KERNEL // 2
    same_doc = segments[:, None] == segments[None, :]
    tap_index = jnp.arange(KERNEL, dtype=jnp.int32)[:, None, None]
    return ((offsets[None] == tap_index) & same_doc[None]).astype(jnp.float32)


def normalize(rows_in):
    widened = rows_in.astype(jnp.float32)
    row_mean = jnp.mean(widened, axis=-1, keepdims=True)
    centred = widened - row_mean
    inv_std = lax.rsqrt(jnp.mean(centred * centred, axis=-1, keepdims=True) + 1e-05)
    normed = centred * inv_std
    return (normed, inv_std, normed.astype(jnp.bfloat16))


def forward_pieces(normed_b, band_table, weights):
    w_value, w_gate, w_kernel = weights
    row_count = normed_b.shape[0]
    value_proj = jnp.dot(normed_b, w_value, preferred_element_type=jnp.float32)
    gate_proj = jnp.dot(normed_b, w_gate, preferred_element_type=jnp.float32)
    gate_sig = jax.nn.sigmoid(gate_proj)
    gated = (value_proj * gate_sig).astype(jnp.bfloat16)
    head_count = w_kernel.shape[1] // KERNEL
    head_size = w_value.shape[1] // head_count
    logits = jnp.dot(normed_b, w_kernel, preferred_element_type=jnp.float32).reshape(
        row_count, head_count, KERNEL
    )
    exp_logits = jnp.exp(logits)
    taps = exp_logits / jnp.sum(exp_logits, axis=-1, keepdims=True)
    band_mat = jnp.einsum(
        "thj,jts->hts",
        taps.astype(jnp.bfloat16),
        band_table.astype(jnp.bfloat16),
        preferred_element_type=jnp.float32,
    ).astype(jnp.bfloat16)
    gated3 = gated.reshape(row_count, head_count, head_size)
    mixed = jnp.einsum(
        "hts,shd->thd", band_mat, gated3, preferred_element_type=jnp.float32
    ).reshape(row_count, -1)
    return (value_proj, gate_sig, gated3, taps, band_mat, mixed)


def layer_forward(full_rows, segments, weights, mp_index):
    normed, inv_std, normed_b = normalize(full_rows)
    pieces = forward_pieces(normed_b, make_table(segments), weights)
    half_width = weights[0].shape[1]
    own_part = lax.dynamic_slice_in_dim(
        full_rows.astype(jnp.float32), mp_index * half_width, half_width, 1
    )
    return (own_part + pieces[5]).astype(jnp.bfloat16)


def layer_backward(normed_b, segments, grad_out, weights):
    w_value, w_gate, w_kernel = weights
    band_table = make_table(segments)
    value_proj, gate_sig, gated3, taps, band_mat, mixed = forward_pieces(
        normed_b, band_table, weights
    )
    row_count, head_count, head_size = gated3.shape
    grad_mixed = grad_out.astype(jnp.bfloat16).reshape(row_count, head_count, head_size)
    grad_gated = jnp.einsum(
        "hts,thd->shd", band_mat, grad_mixed, preferred_element_type=jnp.float32
    ).reshape(row_count, -1)
    tap_outer = jnp.einsum("thd,shd->hts", grad_mixed, gated3, preferred_element_type=jnp.float32)
    grad_taps = jnp.einsum("hts,jts->thj", tap_outer, band_table)
    grad_logits = (
        (taps * (grad_taps - jnp.sum(taps * grad_taps, axis=-1, keepdims=True)))
        .astype(jnp.bfloat16)
        .reshape(row_count, -1)
    )
    grad_value = (grad_gated * gate_sig).astype(jnp.bfloat16)
    grad_gate = (grad_gated * value_proj * gate_sig * (1.0 - gate_sig)).astype(jnp.bfloat16)
    dims = (((1,), (1,)), ((), ()))
    grad_part = lax.dot_general(grad_value, w_value, dims, preferred_element_type=jnp.float32)
    grad_part = grad_part + lax.dot_general(
        grad_gate, w_gate, dims, preferred_element_type=jnp.float32
    )
    grad_part = grad_part + lax.dot_general(
        grad_logits, w_kernel, dims, preferred_element_type=jnp.float32
    )
    return (grad_part, jnp.concatenate([grad_value, grad_gate, grad_logits], axis=1))


def shards(source_rows, value_weight, gate_weight, kernel_weight, segment_ids, out_grad):
    section_count = lax.axis_size("section")
    section_index = lax.axis_index("section")
    mp_index = lax.axis_index("mp")
    micro_count, row_count = segment_ids.shape
    full_width = value_weight.shape[1]
    half_width = value_weight.shape[2]
    weights = (value_weight[0], gate_weight[0], kernel_weight[0])
    term_width = 2 * half_width + kernel_weight.shape[2]
    inputs = source_rows.reshape(micro_count, row_count, half_width)
    top_grads = out_grad.reshape(micro_count, row_count, half_width)
    tick_count = micro_count + section_count - 1

    def forward_tick(tick, carry):
        received, stored = carry
        micro_index = tick - section_index
        active = (micro_index >= 0) & (micro_index < micro_count)
        slot_index = jnp.clip(micro_index, 0, micro_count - 1)
        own_rows = jnp.where(section_index == 0, inputs[slot_index], received)
        full_rows = lax.all_gather(own_rows, "mp", axis=1, tiled=True)
        segments = segment_ids[slot_index]
        result = lax.cond(
            active,
            lambda: layer_forward(full_rows, segments, weights, mp_index),
            lambda: jnp.zeros_like(own_rows),
        )
        stored = stored.at[slot_index].set(jnp.where(active, full_rows, stored[slot_index]))
        passed = from_behind(result, "section", 1)
        return (passed, stored)

    start_rows = jnp.zeros((row_count, half_width), jnp.bfloat16)
    start_store = jnp.zeros((micro_count, row_count, full_width), jnp.bfloat16)
    unused, stored = lax.fori_loop(0, tick_count, forward_tick, (start_rows, start_store))

    def backward_tick(tick, carry):
        received, grads, terms_store = carry
        micro_index = tick - (section_count - 1 - section_index)
        active = (micro_index >= 0) & (micro_index < micro_count)
        slot_index = jnp.clip(micro_index, 0, micro_count - 1)
        top_grad = top_grads[slot_index].astype(jnp.float32)
        grad_out = jnp.where(section_index == section_count - 1, top_grad, received)
        segments = segment_ids[slot_index]
        normed, inv_std, normed_b = normalize(stored[slot_index])
        grad_part, grad_terms = lax.cond(
            active,
            lambda: layer_backward(normed_b, segments, grad_out, weights),
            lambda: (
                jnp.zeros((row_count, full_width), jnp.float32),
                jnp.zeros((row_count, term_width), jnp.bfloat16),
            ),
        )
        grad_normed = lax.psum(grad_part.astype(jnp.bfloat16), "mp").astype(jnp.float32)
        norm_back = inv_std * (
            grad_normed
            - jnp.mean(grad_normed, axis=-1, keepdims=True)
            - normed * jnp.mean(grad_normed * normed, axis=-1, keepdims=True)
        )
        own_back = lax.dynamic_slice_in_dim(norm_back, mp_index * half_width, half_width, 1)
        grad_in = grad_out + own_back
        grad_in = jnp.where(active, grad_in, 0.0)
        grads = lax.cond(
            active,
            lambda: grads
            + lax.dot_general(
                normed_b, grad_terms, (((0,), (0,)), ((), ())), preferred_element_type=jnp.float32
            ),
            lambda: grads,
        )
        passed = from_behind(grad_in.astype(jnp.bfloat16), "section", -1).astype(grad_in.dtype)
        return (passed, grads, terms_store)

    start_grads = jnp.zeros((full_width, term_width), jnp.float32)
    start_terms = jnp.zeros((1,), jnp.bfloat16)
    start_back = jnp.zeros((row_count, half_width), jnp.float32)
    unused, grads, terms_store = lax.fori_loop(
        0, tick_count, backward_tick, (start_back, start_grads, start_terms)
    )
    shares = lax.psum_scatter(
        grads.astype(jnp.bfloat16), "dp", scatter_dimension=0, tiled=True
    ).astype(jnp.float32)
    value_share = shares[:, :half_width][None]
    gate_share = shares[:, half_width : 2 * half_width][None]
    kernel_share = shares[:, 2 * half_width :][None]
    return (value_share, gate_share, kernel_share)


def solution(mesh):
    in_specs = (
        P("dp", "mp"),
        P("section", None, "mp"),
        P("section", None, "mp"),
        P("section", None, "mp"),
        P("dp", None),
        P("dp", "mp"),
    )
    out_specs = (P("section", "dp", "mp"), P("section", "dp", "mp"), P("section", "dp", "mp"))
    return jax.shard_map(shards, mesh=mesh, in_specs=in_specs, out_specs=out_specs, check_vma=False)
```

profile of v0, /device:TPU:0, one launch (start us, length us, event | category | flops | bytes accessed | tf_op | source)
XLA Modules:
  0.0 359.8 jit_solution(7524102810339772016)
XLA Ops:
  8.1 50.1 %while.38 = (s32[]{:T(128)}, bf16[128,256]{0,1:T(8,128)(2,1)S(1)}, bf16[2,128,1024]{1,2,0:T(8,128)(2,1)S(1)}, s32[]{:T(128)}, pred[]{:T(512)}, /*index=5*/bf16[2...) while((s32[]{:T(128)}, bf16[128,256]{0,1:T(8,128)(2,1)S(1)}, ...), condition=%wide.region_7.8_spmd, body=%wide.region_0.7_spmd.sunk | while | flops 184383632 | bytes 11819549 | solution.py:133
  9.1 7.2 %all_gather.9 = bf16[128,1024]{0,1:T(8,128)(2,1)S(1)} all-gather(bf16[128,256]{0,1:T(8,128)(2,1)S(1)} %bitcast_select_fusion.4), channel_id=1, replica_groups=mesh['dp'=4,'section'=2,'mp'=4] {'mp'}, dimensions={1}, use_global_device_ids=true | all-gather | bytes 327680 | tf_op jit(solution)/shard_map/while/body/eval_jaxpr/all_gather | solution.py:120
  16.4 4.1 %conditional.8 = (bf16[128,256]{0,1:T(8,128)(2,1)S(1)}) conditional(s32[]{:T(128)} %convert_element_type.241, () %tuple.133, (bf16[128,1024]{0,1:T(8,128)(2,1)S(1)}, s32[]{:T(128)}, bf16[1024,256]{1,0:T(8,128)(2,1)}, bf16[1024,256]{1,0:T(8,128)(2,1)}, s32[2,128]{1,0:T(2,128)}, /*index=5*/s32[]{:T(128)}, bf16[1024,124]{1,0:T(8,128)(2,1)}) %tuple.134), branch_computations={%region_1.1_spmd, %region_2.5_spmd} | conditional | flops 184088704 | bytes 9459834 | solution.py:122
  24.9 5.8 %all_gather.9 = bf16[128,1024]{0,1:T(8,128)(2,1)S(1)} all-gather(bf16[128,256]{0,1:T(8,128)(2,1)S(1)} %bitcast_select_fusion.4), channel_id=1, replica_groups=mesh['dp'=4,'section'=2,'mp'=4] {'mp'}, dimensions={1}, use_global_device_ids=true | all-gather | bytes 327680 | tf_op jit(solution)/shard_map/while/body/eval_jaxpr/all_gather | solution.py:120
  30.7 4.1 %conditional.8 = (bf16[128,256]{0,1:T(8,128)(2,1)S(1)}) conditional(s32[]{:T(128)} %convert_element_type.241, () %tuple.133, (bf16[128,1024]{0,1:T(8,128)(2,1)S(1)}, s32[]{:T(128)}, bf16[1024,256]{1,0:T(8,128)(2,1)}, bf16[1024,256]{1,0:T(8,128)(2,1)}, s32[2,128]{1,0:T(2,128)}, /*index=5*/s32[]{:T(128)}, bf16[1024,124]{1,0:T(8,128)(2,1)}) %tuple.134), branch_computations={%region_1.1_spmd, %region_2.5_spmd} | conditional | flops 184088704 | bytes 9459834 | solution.py:122
  34.8 4.4 %collective-permute-start = (bf16[128,256]{0,1:T(8,128)(2,1)S(1)}, bf16[128,256]{0,1:T(8,128)(2,1)S(1)}, u32[]{:S(2)}, u32[]{:S(2)}) collective-permute-start(bf16[128,256]{0,1:T(8,128)(2,1)S(1)} %get-tuple-element.1041), channel_id=1, source_target_pairs={{0,4},{1,5},{2,6},{3,7},{8,12},{9,13},{10,14},{11,15},{16,20},{17,... | collective-permute-start | bytes 196616 | tf_op jit(solution)/shard_map/while/body/eval_jaxpr/ppermute | solution.py:12
  42.1 5.8 %all_gather.9 = bf16[128,1024]{0,1:T(8,128)(2,1)S(1)} all-gather(bf16[128,256]{0,1:T(8,128)(2,1)S(1)} %bitcast_select_fusion.4), channel_id=1, replica_groups=mesh['dp'=4,'section'=2,'mp'=4] {'mp'}, dimensions={1}, use_global_device_ids=true | all-gather | bytes 327680 | tf_op jit(solution)/shard_map/while/body/eval_jaxpr/all_gather | solution.py:120
  47.9 8.5 %collective-permute-start = (bf16[128,256]{0,1:T(8,128)(2,1)S(1)}, bf16[128,256]{0,1:T(8,128)(2,1)S(1)}, u32[]{:S(2)}, u32[]{:S(2)}) collective-permute-start(bf16[128,256]{0,1:T(8,128)(2,1)S(1)} %get-tuple-element.1041), channel_id=1, source_target_pairs={{0,4},{1,5},{2,6},{3,7},{8,12},{9,13},{10,14},{11,15},{16,20},{17,... | collective-permute-start | bytes 196616 | tf_op jit(solution)/shard_map/while/body/eval_jaxpr/ppermute | solution.py:12
  59.5 257.4 %while.39 = (s32[]{:T(128)}, f32[128,256]{1,0:T(8,128)}, f32[1024,636]{1,0:T(8,128)S(1)}, s32[]{:T(128)}, pred[]{:T(512)}, /*index=5*/bf16[2,128,256]{2,1,0:T(8,...) while((s32[]{:T(128)}, f32[128,256]{1,0:T(8,128)}, ...), condition=%wide.region_20.21_spmd.clone, body=%wide.region_8.20_spmd.clone.sunk | while | flops 533156512 | bytes 23325744 | solution.py:175
  65.9 71.7 %all-reduce.2.cloned.1.call-done = bf16[128,1024]{1,0:T(8,128)(2,1)} async-done(((bf16[128,1024]{1,0:T(8,128)(2,1)}), bf16[128,1024]{1,0:T(8,128)(2,1)}) %all-reduce.2.cloned.1.call-update) | async-done | bytes 262160 | tf_op jit(solution)/shard_map/while/body/eval_jaxpr/psum | solution.py:152
  141.8 4.8 %collective-permute-done.1 = bf16[128,256]{1,0:T(8,128)(2,1)S(1)} collective-permute-done((bf16[128,256]{1,0:T(8,128)(2,1)S(1)}, bf16[128,256]{1,0:T(8,128)(2,1)S(1)}, u32[]{:S(2)}, u32[]{:S(2)}) %collective-permute-start.1) | collective-permute-done | bytes 65568 | tf_op jit(solution)/shard_map/while/body/eval_jaxpr/ppermute | solution.py:12
  152.3 38.8 %conditional.9 = (bf16[128,1024]{1,0:T(8,128)(2,1)}, bf16[128,636]{1,0:T(8,128)(2,1)}) conditional(s32[]{:T(128)} %convert_element_type.248, () %tuple.138, (s32[2,128]{1,0:T(2,128)}, s32[]{:T(128)}, bf16[128,1024]{1,0:T(8,128)(2,1)}, bf16[1024,124]{1,0:T(8,128)(2,1)}, f32[128,256]{1,0:T(8,128)S(1)}, /*index=5*/bf16[1024,256]{1,0:T(8,128)(2,1)}, ...), branch_computations={%region_11.11_spmd, %region_12.14_spmd} | conditional | flops 362930720 | bytes 10925676 | solution.py:144
  154.5 1.9 convolution_exponential_fusion.1
  160.7 2.0 fusion.23
  168.4 2.0 multiply_convert_fusion.4
  172.0 1.8 convolution_bitcast_fusion
  176.9 7.4 %fusion.20 = bf16[128,4,31]{2,1,0:T(4,128)(2,1)} fusion(f32[128,4,31]{2,1,0:T(4,128)S(1)} %fusion.16, f32[128,4,31]{2,1,0:T(4,128)} %copy.31, f32[128,4]{1,0:T(8,128)} %copy.30), kind=kOutput, calls=%fused_computation.45 | output fusion | flops 95774 | bytes 160768 | tf_op jit(solution)/shard_map/while/body/eval_jaxpr/cond/branch_1_fun/sub | solution.py:84
  191.1 31.2 %all-reduce.2.cloned.1.call-done = bf16[128,1024]{1,0:T(8,128)(2,1)} async-done(((bf16[128,1024]{1,0:T(8,128)(2,1)}), bf16[128,1024]{1,0:T(8,128)(2,1)}) %all-reduce.2.cloned.1.call-update) | async-done | bytes 262160 | tf_op jit(solution)/shard_map/while/body/eval_jaxpr/psum | solution.py:152
  226.6 1.7 conditional.10
  226.6 1.7 convolution_add_fusion.2
  228.3 3.1 collective-permute-done.1
  237.1 38.8 %conditional.9 = (bf16[128,1024]{1,0:T(8,128)(2,1)}, bf16[128,636]{1,0:T(8,128)(2,1)}) conditional(s32[]{:T(128)} %convert_element_type.248, () %tuple.138, (s32[2,128]{1,0:T(2,128)}, s32[]{:T(128)}, bf16[128,1024]{1,0:T(8,128)(2,1)}, bf16[1024,124]{1,0:T(8,128)(2,1)}, f32[128,256]{1,0:T(8,128)S(1)}, /*index=5*/bf16[1024,256]{1,0:T(8,128)(2,1)}, ...), branch_computations={%region_11.11_spmd, %region_12.14_spmd} | conditional | flops 362930720 | bytes 10925676 | solution.py:144
  239.3 1.9 convolution_exponential_fusion.1
  245.5 2.0 fusion.23
  253.2 2.0 multiply_convert_fusion.4
  256.8 1.8 convolution_bitcast_fusion
  261.7 7.4 %fusion.20 = bf16[128,4,31]{2,1,0:T(4,128)(2,1)} fusion(f32[128,4,31]{2,1,0:T(4,128)S(1)} %fusion.16, f32[128,4,31]{2,1,0:T(4,128)} %copy.31, f32[128,4]{1,0:T(8,128)} %copy.30), kind=kOutput, calls=%fused_computation.45 | output fusion | flops 95774 | bytes 160768 | tf_op jit(solution)/shard_map/while/body/eval_jaxpr/cond/branch_1_fun/sub | solution.py:84
  275.9 31.2 %all-reduce.2.cloned.1.call-done = bf16[128,1024]{1,0:T(8,128)(2,1)} async-done(((bf16[128,1024]{1,0:T(8,128)(2,1)}), bf16[128,1024]{1,0:T(8,128)(2,1)}) %all-reduce.2.cloned.1.call-update) | async-done | bytes 262160 | tf_op jit(solution)/shard_map/while/body/eval_jaxpr/psum | solution.py:152
  311.4 1.7 conditional.10
  311.4 1.7 convolution_add_fusion.2
  313.1 3.1 collective-permute-done.1
  318.2 31.9 %reduce-scatter.2.cloned.1.call-done = bf16[256,636]{1,0:T(8,128)(2,1)} async-done(((bf16[1024,636]{1,0:T(8,128)(2,1)}), bf16[256,636]{1,0:T(8,128)(2,1)}) %reduce-scatter.2.cloned.1.call-update) | async-done | bytes 325648 | tf_op jit(solution)/shard_map/reduce_scatter | solution.py:178
  (205 shorter events, 102.9 us)
Async XLA Ops:
  16.4 5.5 %copy-start.9 = (s32[3]{0:T(128)S(1)}, s32[3]{0:T(128)}, u32[]{:S(2)}) copy-start(s32[3]{0:T(128)} %get-tuple-element.994) | copy-start | bytes 40 | tf_op jit(solution)/shard_map/while
  16.4 3.2 copy-start
  16.4 3.4 copy-start.5
  20.5 3.4 collective-permute-start
  30.7 8.6 %copy-start.9 = (s32[3]{0:T(128)S(1)}, s32[3]{0:T(128)}, u32[]{:S(2)}) copy-start(s32[3]{0:T(128)} %get-tuple-element.994) | copy-start | bytes 40 | tf_op jit(solution)/shard_map/while
  30.7 3.2 copy-start
  30.7 3.4 copy-start.5
  34.8 6.3 %collective-permute-start = (bf16[128,256]{0,1:T(8,128)(2,1)S(1)}, bf16[128,256]{0,1:T(8,128)(2,1)S(1)}, u32[]{:S(2)}, u32[]{:S(2)}) collective-permute-start(bf16[128,256]{0,1:T(8,128)(2,1)S(1)} %get-tuple-element.1041), channel_id=1, source_target_pairs={{0,4},{1,5},{2,6},{3,7},{8,12},{9,13},{10,14},{11,15},{16,20},{17,... | collective-permute-start | bytes 196616 | tf_op jit(solution)/shard_map/while/body/eval_jaxpr/ppermute | solution.py:12
  47.9 8.5 %copy-start.9 = (s32[3]{0:T(128)S(1)}, s32[3]{0:T(128)}, u32[]{:S(2)}) copy-start(s32[3]{0:T(128)} %get-tuple-element.994) | copy-start | bytes 40 | tf_op jit(solution)/shard_map/while
  47.9 10.4 %collective-permute-start = (bf16[128,256]{0,1:T(8,128)(2,1)S(1)}, bf16[128,256]{0,1:T(8,128)(2,1)S(1)}, u32[]{:S(2)}, u32[]{:S(2)}) collective-permute-start(bf16[128,256]{0,1:T(8,128)(2,1)S(1)} %get-tuple-element.1041), channel_id=1, source_target_pairs={{0,4},{1,5},{2,6},{3,7},{8,12},{9,13},{10,14},{11,15},{16,20},{17,... | collective-permute-start | bytes 196616 | tf_op jit(solution)/shard_map/while/body/eval_jaxpr/ppermute | solution.py:12
  58.3 0.8 copy-start.3
  58.3 1.2 copy-start.1
  59.5 78.1 %all-reduce.2.cloned.1.call-start = ((), (), s32[]{:S(2)}) async-start(), calls=%async_computation.2 | async-start | bytes 524288 | tf_op jit(solution)/shard_map/while/body/eval_jaxpr/psum | solution.py:152
  62.4 1.2 copy-start.7
  62.6 0.9 copy-start.8
  140.5 6.2 %collective-permute-start.1 = (bf16[128,256]{1,0:T(8,128)(2,1)S(1)}, bf16[128,256]{1,0:T(8,128)(2,1)S(1)}, u32[]{:S(2)}, u32[]{:S(2)}) collective-permute-start(bf16[128,256]{1,0:T(8,128)(2,1)S(1)} %fusion.74), channel_id=1, source_target_pairs={{4,0},{5,1},{6,2},{7,3},{12,8},{13,9},{14,10},{15,11},{20,16},{21,... | collective-permute-start | bytes 196616 | tf_op jit(solution)/shard_map/while/body/eval_jaxpr/ppermute | solution.py:12
  147.3 75.0 %all-reduce.2.cloned.1.call-start = ((), (), s32[]{:S(2)}) async-start(), calls=%async_computation.2 | async-start | bytes 524288 | tf_op jit(solution)/shard_map/while/body/eval_jaxpr/psum | solution.py:152
  150.2 1.2 copy-start.7
  150.5 0.9 copy-start.8
  164.4 1.5 copy-start.4
  186.0 4.2 %copy-start.2 = (bf16[1024,124]{1,0:T(8,128)(2,1)S(1)}, bf16[1024,124]{1,0:T(8,128)(2,1)}, u32[]{:S(2)}) copy-start(bf16[1024,124]{1,0:T(8,128)(2,1)} %get-tuple-element.579) | copy-start | bytes 761860 | tf_op jit(solution)/shard_map/while/body/eval_jaxpr/cond
  186.0 4.2 %copy-start.6 = (bf16[128,124]{1,0:T(8,128)(2,1)S(1)}, bf16[128,124]{1,0:T(8,128)(2,1)}, u32[]{:S(2)}) copy-start(bf16[128,124]{1,0:T(8,128)(2,1)} %reshape.248) | copy-start | bytes 95236 | tf_op jit(solution)/shard_map/while/body/eval_jaxpr/cond
  225.3 6.2 %collective-permute-start.1 = (bf16[128,256]{1,0:T(8,128)(2,1)S(1)}, bf16[128,256]{1,0:T(8,128)(2,1)S(1)}, u32[]{:S(2)}, u32[]{:S(2)}) collective-permute-start(bf16[128,256]{1,0:T(8,128)(2,1)S(1)} %fusion.74), channel_id=1, source_target_pairs={{4,0},{5,1},{6,2},{7,3},{12,8},{13,9},{14,10},{15,11},{20,16},{21,... | collective-permute-start | bytes 196616 | tf_op jit(solution)/shard_map/while/body/eval_jaxpr/ppermute | solution.py:12
  232.1 75.0 %all-reduce.2.cloned.1.call-start = ((), (), s32[]{:S(2)}) async-start(), calls=%async_computation.2 | async-start | bytes 524288 | tf_op jit(solution)/shard_map/while/body/eval_jaxpr/psum | solution.py:152
  235.0 1.2 copy-start.7
  235.3 0.9 copy-start.8
  249.2 1.5 copy-start.4
  270.8 4.2 %copy-start.2 = (bf16[1024,124]{1,0:T(8,128)(2,1)S(1)}, bf16[1024,124]{1,0:T(8,128)(2,1)}, u32[]{:S(2)}) copy-start(bf16[1024,124]{1,0:T(8,128)(2,1)} %get-tuple-element.579) | copy-start | bytes 761860 | tf_op jit(solution)/shard_map/while/body/eval_jaxpr/cond
  270.8 4.2 %copy-start.6 = (bf16[128,124]{1,0:T(8,128)(2,1)S(1)}, bf16[128,124]{1,0:T(8,128)(2,1)}, u32[]{:S(2)}) copy-start(bf16[128,124]{1,0:T(8,128)(2,1)} %reshape.248) | copy-start | bytes 95236 | tf_op jit(solution)/shard_map/while/body/eval_jaxpr/cond
  310.1 6.2 %collective-permute-start.1 = (bf16[128,256]{1,0:T(8,128)(2,1)S(1)}, bf16[128,256]{1,0:T(8,128)(2,1)S(1)}, u32[]{:S(2)}, u32[]{:S(2)}) collective-permute-start(bf16[128,256]{1,0:T(8,128)(2,1)S(1)} %fusion.74), channel_id=1, source_target_pairs={{4,0},{5,1},{6,2},{7,3},{12,8},{13,9},{14,10},{15,11},{20,16},{21,... | collective-permute-start | bytes 196616 | tf_op jit(solution)/shard_map/while/body/eval_jaxpr/ppermute | solution.py:12
  316.9 33.1 %reduce-scatter.2.cloned.1.call-start = ((), (), s32[]{:S(2)}) async-start(), calls=%async_computation.1 | async-start | bytes 1638400 | tf_op jit(solution)/shard_map/reduce_scatter | solution.py:178
Sparse Core Ops, SparseCore 0:
  66.0 71.5 all-reduce.1
  191.3 31.0 all-reduce.1
  276.0 31.0 all-reduce.1
Sparse Core Ops, SparseCore 1:
  319.7 30.3 reduce-scatter.1
where the time goes:
time: 362 us; the launch traced here: 360 us
  waiting for transfers between devices  179 us (49%)
  other arithmetic  47.1 us (13%)
  local copies, waits for them, and re-layouts  42.7 us (12%)
  matrix products  38.4 us (11%)
  blocking collectives  18.8 us (5%)
  starting transfers between devices  18 us (5%)
  between operations  15.2 us (4%)
    psum x3, waiting for transfers between devices, backward_tick(): lax.psum(grad_part.astype(jnp.bfloat16), 'mp').astype(jnp.float32)  134 us
    reduce_scatter x1, waiting for transfers between devices, shards(): lax.psum_scatter(grads.astype(jnp.bfloat16), 'dp', scatter_dimension=0, t...  31.9 us
    all_gather x3, blocking collectives, forward_tick(): full_rows = lax.all_gather(own_rows, 'mp', axis=1, tiled=True)  18.8 us
    ppermute x6, starting transfers between devices, from_behind(): lax.ppermute(value, axis, [(source, source + steps) for source in range(i...  18 us
    sub x2, other arithmetic, layer_backward(): grad_taps - jnp.sum(taps * grad_taps, axis=-1, keepdims=True)  14.8 us
    ppermute x6, waiting for transfers between devices, from_behind(): lax.ppermute(value, axis, [(source, source + steps) for source in range(i...  12.7 us
    dynamic_slice x6, local copies, waits for them, and re-layouts, backward_tick(): normed, inv_std, normed_b = normalize(stored[slot_index])  8.26 us
  transfers between devices with their start and end apart: 10, of which 10 were waited for; matrix products, arithmetic and copies ran while one was open for 2% of the time, Pallas kernels for 0%

commit v1 on v0

--- a/solution.py
+++ b/solution.py
@@ -4,6 +4,24 @@
 from jax.sharding import PartitionSpec as P
 
 KERNEL = 31
+
+
+def in_order(blocks, dim):
+    blocks = jnp.moveaxis(blocks, 0, dim)
+    shape = blocks.shape
+    return blocks.reshape(*shape[:dim], shape[dim] * shape[dim + 1], *shape[dim + 2 :])
+
+
+def grow_blocks(x, axis):
+    count = lax.axis_size(axis)
+    pieces = x[None]
+    for level in range(count.bit_length() - 1):
+        bit = 1 << level
+        other = lax.ppermute(pieces, axis, [(i, i ^ bit) for i in range(count)])
+        both = jnp.stack([pieces, other])
+        upper = lax.axis_index(axis) >> level & 1
+        pieces = jnp.where(upper == 0, both, both[::-1]).reshape(-1, *x.shape)
+    return pieces
 
 
 def from_behind(value, axis, steps):
@@ -117,7 +135,7 @@
         active = (micro_index >= 0) & (micro_index < micro_count)
         slot_index = jnp.clip(micro_index, 0, micro_count - 1)
         own_rows = jnp.where(section_index == 0, inputs[slot_index], received)
-        full_rows = lax.all_gather(own_rows, "mp", axis=1, tiled=True)
+        full_rows = in_order(grow_blocks(own_rows, "mp"), 1)
         segments = segment_ids[slot_index]
         result = lax.cond(
             active,

time: 362 us -> 373 us (1.030)
  blocking collectives: 18.8 us -> 0 us
  other arithmetic: 47.1 us -> 64.2 us
  waiting for transfers between devices: 179 us -> 192 us
  starting transfers between devices: 18 us -> 26.6 us
  local copies, waits for them, and re-layouts: 42.7 us -> 36.2 us
    all_gather x3 -> x0, blocking collectives: 18.8 us -> none  [forward_tick(): full_rows = lax.all_gather(own_rows, 'mp', axis=1, tiled=True)]
    ppermute x0 -> x6, waiting for transfers between devices: none -> 10.6 us  [grow_blocks(): other = lax.ppermute(pieces, axis, [(i, i ^ bit) for i in range(count)])]
    dynamic_slice x9 -> x0, local copies, waits for them, and re-layouts: 8.34 us -> none  [the longest x6 8.26 us: backward_tick(): normed, inv_std, normed_b = normalize(stored[slot_index])]
    ppermute x0 -> x6, starting transfers between devices: none -> 7.2 us  [grow_blocks(): other = lax.ppermute(pieces, axis, [(i, i ^ bit) for i in range(count)])]
    reduce_sum x5, other arithmetic: 0.96 us -> 7.26 us  [normalize(): jnp.mean(centred * centred, axis=-1, keepdims=True) + 1e-05]
    reduce_sum x5, other arithmetic: 0.65 us -> 5.26 us  [normalize(): row_mean = jnp.mean(widened, axis=-1, keepdims=True)]
  transfers between devices with their start and end apart: 10 -> 16, of which waited for: 10 -> 16; matrix products, arithmetic and copies ran while one was open for 2% -> 3% of each run, Pallas kernels for 0% -> 0%
where the time goes in v1:
time: 373 us; the launch traced here: 371 us
  waiting for transfers between devices  192 us (51%)
  other arithmetic  64.2 us (17%)
  local copies, waits for them, and re-layouts  36.2 us (10%)
  matrix products  35.8 us (10%)
  starting transfers between devices  26.6 us (7%)
  between operations  15.2 us (4%)
    psum x3, waiting for transfers between devices, backward_tick(): lax.psum(grad_part.astype(jnp.bfloat16), 'mp').astype(jnp.float32)  134 us
    reduce_scatter x1, waiting for transfers between devices, shards(): lax.psum_scatter(grads.astype(jnp.bfloat16), 'dp', scatter_dimension=0, t...  31.9 us
    ppermute x6, starting transfers between devices, from_behind(): lax.ppermute(value, axis, [(source, source + steps) for source in range(i...  19.4 us
    ppermute x6, waiting for transfers between devices, from_behind(): lax.ppermute(value, axis, [(source, source + steps) for source in range(i...  15.3 us
    sub x2, other arithmetic, layer_backward(): grad_taps - jnp.sum(taps * grad_taps, axis=-1, keepdims=True)  14.7 us
    ppermute x6, waiting for transfers between devices, grow_blocks(): other = lax.ppermute(pieces, axis, [(i, i ^ bit) for i in range(count)])  10.6 us
  transfers between devices with their start and end apart: 16, of which 16 were waited for; matrix products, arithmetic and copies ran while one was open for 3% of the time, Pallas kernels for 0%

profile of v1, /device:TPU:0, one launch (start us, length us, event | category | flops | bytes accessed | tf_op | source)
XLA Modules:
  0.0 370.9 jit_solution(9619249611985128554)
XLA Ops:
  9.2 59.7 %while.38 = (s32[]{:T(128)}, bf16[128,256]{0,1:T(8,128)(2,1)S(1)}, bf16[2,128,1024]{2,1,0:T(8,128)(2,1)S(1)}, s32[]{:T(128)}, pred[]{:T(512)}, /*index=5*/bf16[2...) while((s32[]{:T(128)}, bf16[128,256]{0,1:T(8,128)(2,1)S(1)}, ...), condition=%wide.region_7.8_spmd, body=%wide.region_0.7_spmd.sunk | while | flops 184383648 | bytes 16466581 | solution.py:151
  11.8 2.9 collective-permute-start.1
  16.2 2.4 collective-permute-done.1
  19.1 5.7 %conditional.8 = (bf16[128,256]{0,1:T(8,128)(2,1)S(1)}) conditional(s32[]{:T(128)} %convert_element_type.252, () %tuple.138, (bf16[128,4,256]{2,1,0:T(4,128)(2,1)S(1)}, s32[]{:T(128)}, bf16[1024,256]{1,0:T(8,128)(2,1)S(1)}, bf16[1024,256]{1,0:T(8,128)(2,1)S(1)}, s32[2,128]{1,0:T(2,128)S(1)}, /*index=5*/s32[]{:T(128)}, ...), branch_computations={%region_1.1_spmd, %region_2.5_spmd} | conditional | flops 183695488 | bytes 7155774 | solution.py:140
  20.2 1.9 multiply_reduce_fusion
  30.5 1.8 collective-permute-start.1
  33.7 2.4 collective-permute-done.1
  36.6 5.7 %conditional.8 = (bf16[128,256]{0,1:T(8,128)(2,1)S(1)}) conditional(s32[]{:T(128)} %convert_element_type.252, () %tuple.138, (bf16[128,4,256]{2,1,0:T(4,128)(2,1)S(1)}, s32[]{:T(128)}, bf16[1024,256]{1,0:T(8,128)(2,1)S(1)}, bf16[1024,256]{1,0:T(8,128)(2,1)S(1)}, s32[2,128]{1,0:T(2,128)S(1)}, /*index=5*/s32[]{:T(128)}, ...), branch_computations={%region_1.1_spmd, %region_2.5_spmd} | conditional | flops 183695488 | bytes 7155774 | solution.py:140
  37.7 1.9 multiply_reduce_fusion
  42.3 4.3 %collective-permute-start.2 = (bf16[128,256]{0,1:T(8,128)(2,1)S(1)}, bf16[128,256]{0,1:T(8,128)(2,1)S(1)}, u32[]{:S(2)}, u32[]{:S(2)}) collective-permute-start(bf16[128,256]{0,1:T(8,128)(2,1)S(1)} %get-tuple-element.1034), channel_id=1, source_target_pairs={{0,4},{1,5},{2,6},{3,7},{8,12},{9,13},{10,14},{11,15},{16,20},{17,... | collective-permute-start | bytes 196616 | tf_op jit(solution)/shard_map/while/body/eval_jaxpr/ppermute | solution.py:30
  51.0 1.8 collective-permute-start.1
  54.2 2.4 collective-permute-done.1
  57.1 10.0 %collective-permute-start.2 = (bf16[128,256]{0,1:T(8,128)(2,1)S(1)}, bf16[128,256]{0,1:T(8,128)(2,1)S(1)}, u32[]{:S(2)}, u32[]{:S(2)}) collective-permute-start(bf16[128,256]{0,1:T(8,128)(2,1)S(1)} %get-tuple-element.1034), channel_id=1, source_target_pairs={{0,4},{1,5},{2,6},{3,7},{8,12},{9,13},{10,14},{11,15},{16,20},{17,... | collective-permute-start | bytes 196616 | tf_op jit(solution)/shard_map/while/body/eval_jaxpr/ppermute | solution.py:30
  70.2 257.9 %while.39 = (s32[]{:T(128)}, f32[128,256]{1,0:T(8,128)}, f32[1024,636]{1,0:T(8,128)S(1)}, s32[]{:T(128)}, pred[]{:T(512)}, /*index=5*/bf16[2,128,256]{2,1,0:T(8,...) while((s32[]{:T(128)}, f32[128,256]{1,0:T(8,128)}, ...), condition=%wide.region_20.21_spmd.clone, body=%wide.region_8.20_spmd.clone.sunk | while | flops 533156512 | bytes 22277180 | solution.py:193
  76.0 71.5 %all-reduce.2.cloned.1.call-done = bf16[128,1024]{1,0:T(8,128)(2,1)} async-done(((bf16[128,1024]{1,0:T(8,128)(2,1)}), bf16[128,1024]{1,0:T(8,128)(2,1)}) %all-reduce.2.cloned.1.call-update) | async-done | bytes 262160 | tf_op jit(solution)/shard_map/while/body/eval_jaxpr/psum | solution.py:170
  152.5 5.0 %collective-permute-done.3 = bf16[128,256]{1,0:T(8,128)(2,1)S(1)} collective-permute-done((bf16[128,256]{1,0:T(8,128)(2,1)}, bf16[128,256]{1,0:T(8,128)(2,1)S(1)}, u32[]{:S(2)}, u32[]{:S(2)}) %collective-permute-start.3) | collective-permute-done | bytes 65568 | tf_op jit(solution)/shard_map/while/body/eval_jaxpr/ppermute | solution.py:30
  162.7 38.5 %conditional.9 = (bf16[128,1024]{1,0:T(8,128)(2,1)}, bf16[128,636]{1,0:T(8,128)(2,1)}) conditional(s32[]{:T(128)} %convert_element_type.259, () %tuple.143, (s32[2,128]{1,0:T(2,128)}, s32[]{:T(128)}, bf16[128,1024]{1,0:T(8,128)(2,1)S(1)}, bf16[1024,124]{1,0:T(8,128)(2,1)}, f32[128,256]{1,0:T(8,128)S(1)}, /*index=5*/bf16[1024,256]{1,0:T(8,128)(2,1)}, ...), branch_computations={%region_11.11_spmd, %region_12.14_spmd} | conditional | flops 362930720 | bytes 10925676 | solution.py:162
  164.8 1.9 convolution_exponential_fusion.1
  171.0 1.9 fusion.27
  178.6 1.9 multiply_convert_fusion.4
  182.1 1.8 convolution_bitcast_fusion
  187.1 7.3 %fusion.24 = bf16[128,4,31]{2,1,0:T(4,128)(2,1)} fusion(f32[128,4,31]{2,1,0:T(4,128)S(1)} %fusion.20, f32[128,4,31]{2,1,0:T(4,128)} %copy.37, f32[128,4]{1,0:T(8,128)} %copy.36), kind=kOutput, calls=%fused_computation.52 | output fusion | flops 95774 | bytes 160768 | tf_op jit(solution)/shard_map/while/body/eval_jaxpr/cond/branch_1_fun/sub | solution.py:102
  201.2 31.2 %all-reduce.2.cloned.1.call-done = bf16[128,1024]{1,0:T(8,128)(2,1)} async-done(((bf16[128,1024]{1,0:T(8,128)(2,1)}), bf16[128,1024]{1,0:T(8,128)(2,1)}) %all-reduce.2.cloned.1.call-update) | async-done | bytes 262160 | tf_op jit(solution)/shard_map/while/body/eval_jaxpr/psum | solution.py:170
  239.1 3.4 collective-permute-done.3
  247.6 38.5 %conditional.9 = (bf16[128,1024]{1,0:T(8,128)(2,1)}, bf16[128,636]{1,0:T(8,128)(2,1)}) conditional(s32[]{:T(128)} %convert_element_type.259, () %tuple.143, (s32[2,128]{1,0:T(2,128)}, s32[]{:T(128)}, bf16[128,1024]{1,0:T(8,128)(2,1)S(1)}, bf16[1024,124]{1,0:T(8,128)(2,1)}, f32[128,256]{1,0:T(8,128)S(1)}, /*index=5*/bf16[1024,256]{1,0:T(8,128)(2,1)}, ...), branch_computations={%region_11.11_spmd, %region_12.14_spmd} | conditional | flops 362930720 | bytes 10925676 | solution.py:162
  249.7 1.9 convolution_exponential_fusion.1
  255.9 1.9 fusion.27
  263.5 1.9 multiply_convert_fusion.4
  271.9 7.3 %fusion.24 = bf16[128,4,31]{2,1,0:T(4,128)(2,1)} fusion(f32[128,4,31]{2,1,0:T(4,128)S(1)} %fusion.20, f32[128,4,31]{2,1,0:T(4,128)} %copy.37, f32[128,4]{1,0:T(8,128)} %copy.36), kind=kOutput, calls=%fused_computation.52 | output fusion | flops 95774 | bytes 160768 | tf_op jit(solution)/shard_map/while/body/eval_jaxpr/cond/branch_1_fun/sub | solution.py:102
  286.1 31.2 %all-reduce.2.cloned.1.call-done = bf16[128,1024]{1,0:T(8,128)(2,1)} async-done(((bf16[128,1024]{1,0:T(8,128)(2,1)}), bf16[128,1024]{1,0:T(8,128)(2,1)}) %all-reduce.2.cloned.1.call-update) | async-done | bytes 262160 | tf_op jit(solution)/shard_map/while/body/eval_jaxpr/psum | solution.py:170
  324.0 3.4 collective-permute-done.3
  329.3 31.9 %reduce-scatter.2.cloned.1.call-done = bf16[256,636]{1,0:T(8,128)(2,1)} async-done(((bf16[1024,636]{1,0:T(8,128)(2,1)}), bf16[256,636]{1,0:T(8,128)(2,1)}) %reduce-scatter.2.cloned.1.call-update) | async-done | bytes 325648 | tf_op jit(solution)/shard_map/reduce_scatter | solution.py:196
  (230 shorter events, 122.1 us)
Async XLA Ops:
  9.2 9.8 %copy-start = (bf16[1024,256]{1,0:T(8,128)(2,1)S(1)}, bf16[1024,256]{1,0:T(8,128)(2,1)}, u32[]{:S(2)}) copy-start(bf16[1024,256]{1,0:T(8,128)(2,1)} %get-tuple-element.979) | copy-start | bytes 1572868 | tf_op jit(solution)/shard_map/while
  9.2 9.8 %copy-start.3 = (bf16[1024,256]{1,0:T(8,128)(2,1)S(1)}, bf16[1024,256]{1,0:T(8,128)(2,1)}, u32[]{:S(2)}) copy-start(bf16[1024,256]{1,0:T(8,128)(2,1)} %get-tuple-element.980) | copy-start | bytes 1572868 | tf_op jit(solution)/shard_map/while
  9.3 9.8 %copy-start.9 = (s32[2,128]{1,0:T(2,128)S(1)}, s32[2,128]{1,0:T(2,128)}, u32[]{:S(2)}) copy-start(s32[2,128]{1,0:T(2,128)} %get-tuple-element.981) | copy-start | bytes 3076 | tf_op jit(solution)/shard_map/while
  10.3 1.4 collective-permute-start
  11.8 6.8 %collective-permute-start.1 = (bf16[2,128,256]{1,2,0:T(8,128)(2,1)S(1)}, bf16[2,128,256]{1,2,0:T(8,128)(2,1)S(1)}, u32[]{:S(2)}, u32[]{:S(2)}) collective-permute-start(bf16[2,128,256]{1,2,0:T(8,128)(2,1)S(1)} %get-tuple-element.913), channel_id=1, source_target_pairs={{0,2},{1,3},{2,0},{3,1},{4,6},{5,7},{6,4},{7,5},{8,10},{9,11},{10,... | collective-permute-start | bytes 393224 | tf_op jit(solution)/shard_map/while/body/eval_jaxpr/ppermute | solution.py:20
  24.8 3.2 collective-permute-start.2
  28.0 8.6 %copy-start = (bf16[1024,256]{1,0:T(8,128)(2,1)S(1)}, bf16[1024,256]{1,0:T(8,128)(2,1)}, u32[]{:S(2)}) copy-start(bf16[1024,256]{1,0:T(8,128)(2,1)} %get-tuple-element.979) | copy-start | bytes 1572868 | tf_op jit(solution)/shard_map/while
  28.0 8.6 %copy-start.3 = (bf16[1024,256]{1,0:T(8,128)(2,1)S(1)}, bf16[1024,256]{1,0:T(8,128)(2,1)}, u32[]{:S(2)}) copy-start(bf16[1024,256]{1,0:T(8,128)(2,1)} %get-tuple-element.980) | copy-start | bytes 1572868 | tf_op jit(solution)/shard_map/while
  28.0 8.6 %copy-start.9 = (s32[2,128]{1,0:T(2,128)S(1)}, s32[2,128]{1,0:T(2,128)}, u32[]{:S(2)}) copy-start(s32[2,128]{1,0:T(2,128)} %get-tuple-element.981) | copy-start | bytes 3076 | tf_op jit(solution)/shard_map/while
  29.1 1.3 collective-permute-start
  30.5 5.6 %collective-permute-start.1 = (bf16[2,128,256]{1,2,0:T(8,128)(2,1)S(1)}, bf16[2,128,256]{1,2,0:T(8,128)(2,1)S(1)}, u32[]{:S(2)}, u32[]{:S(2)}) collective-permute-start(bf16[2,128,256]{1,2,0:T(8,128)(2,1)S(1)} %get-tuple-element.913), channel_id=1, source_target_pairs={{0,2},{1,3},{2,0},{3,1},{4,6},{5,7},{6,4},{7,5},{8,10},{9,11},{10,... | collective-permute-start | bytes 393224 | tf_op jit(solution)/shard_map/while/body/eval_jaxpr/ppermute | solution.py:20
  42.3 6.2 %collective-permute-start.2 = (bf16[128,256]{0,1:T(8,128)(2,1)S(1)}, bf16[128,256]{0,1:T(8,128)(2,1)S(1)}, u32[]{:S(2)}, u32[]{:S(2)}) collective-permute-start(bf16[128,256]{0,1:T(8,128)(2,1)S(1)} %get-tuple-element.1034), channel_id=1, source_target_pairs={{0,4},{1,5},{2,6},{3,7},{8,12},{9,13},{10,14},{11,15},{16,20},{17,... | collective-permute-start | bytes 196616 | tf_op jit(solution)/shard_map/while/body/eval_jaxpr/ppermute | solution.py:30
  48.5 8.6 %copy-start = (bf16[1024,256]{1,0:T(8,128)(2,1)S(1)}, bf16[1024,256]{1,0:T(8,128)(2,1)}, u32[]{:S(2)}) copy-start(bf16[1024,256]{1,0:T(8,128)(2,1)} %get-tuple-element.979) | copy-start | bytes 1572868 | tf_op jit(solution)/shard_map/while
  48.5 8.6 %copy-start.3 = (bf16[1024,256]{1,0:T(8,128)(2,1)S(1)}, bf16[1024,256]{1,0:T(8,128)(2,1)}, u32[]{:S(2)}) copy-start(bf16[1024,256]{1,0:T(8,128)(2,1)} %get-tuple-element.980) | copy-start | bytes 1572868 | tf_op jit(solution)/shard_map/while
  48.5 8.6 %copy-start.9 = (s32[2,128]{1,0:T(2,128)S(1)}, s32[2,128]{1,0:T(2,128)}, u32[]{:S(2)}) copy-start(s32[2,128]{1,0:T(2,128)} %get-tuple-element.981) | copy-start | bytes 3076 | tf_op jit(solution)/shard_map/while
  49.6 1.3 collective-permute-start
  51.0 5.6 %collective-permute-start.1 = (bf16[2,128,256]{1,2,0:T(8,128)(2,1)S(1)}, bf16[2,128,256]{1,2,0:T(8,128)(2,1)S(1)}, u32[]{:S(2)}, u32[]{:S(2)}) collective-permute-start(bf16[2,128,256]{1,2,0:T(8,128)(2,1)S(1)} %get-tuple-element.913), channel_id=1, source_target_pairs={{0,2},{1,3},{2,0},{3,1},{4,6},{5,7},{6,4},{7,5},{8,10},{9,11},{10,... | collective-permute-start | bytes 393224 | tf_op jit(solution)/shard_map/while/body/eval_jaxpr/ppermute | solution.py:20
  57.1 11.8 %collective-permute-start.2 = (bf16[128,256]{0,1:T(8,128)(2,1)S(1)}, bf16[128,256]{0,1:T(8,128)(2,1)S(1)}, u32[]{:S(2)}, u32[]{:S(2)}) collective-permute-start(bf16[128,256]{0,1:T(8,128)(2,1)S(1)} %get-tuple-element.1034), channel_id=1, source_target_pairs={{0,4},{1,5},{2,6},{3,7},{8,12},{9,13},{10,14},{11,15},{16,20},{17,... | collective-permute-start | bytes 196616 | tf_op jit(solution)/shard_map/while/body/eval_jaxpr/ppermute | solution.py:30
  70.2 77.3 %all-reduce.2.cloned.1.call-start = ((), (), s32[]{:S(2)}) async-start(), calls=%async_computation.2 | async-start | bytes 524288 | tf_op jit(solution)/shard_map/while/body/eval_jaxpr/psum | solution.py:170
  71.3 3.2 copy-start.7
  151.2 6.4 %collective-permute-start.3 = (bf16[128,256]{1,0:T(8,128)(2,1)}, bf16[128,256]{1,0:T(8,128)(2,1)S(1)}, u32[]{:S(2)}, u32[]{:S(2)}) collective-permute-start(bf16[128,256]{1,0:T(8,128)(2,1)} %fusion.84), channel_id=1, source_target_pairs={{4,0},{5,1},{6,2},{7,3},{12,8},{13,9},{14,10},{15,11},{20,16},{21,... | collective-permute-start | bytes 196616 | tf_op jit(solution)/shard_map/while/body/eval_jaxpr/ppermute | solution.py:30
  158.3 74.1 %all-reduce.2.cloned.1.call-start = ((), (), s32[]{:S(2)}) async-start(), calls=%async_computation.2 | async-start | bytes 524288 | tf_op jit(solution)/shard_map/while/body/eval_jaxpr/psum | solution.py:170
  159.3 3.3 copy-start.7
  196.0 4.2 %copy-start.4 = (bf16[1024,124]{1,0:T(8,128)(2,1)S(1)}, bf16[1024,124]{1,0:T(8,128)(2,1)}, u32[]{:S(2)}) copy-start(bf16[1024,124]{1,0:T(8,128)(2,1)} %get-tuple-element.580) | copy-start | bytes 761860 | tf_op jit(solution)/shard_map/while/body/eval_jaxpr/cond
  196.1 4.2 %copy-start.6 = (bf16[128,124]{1,0:T(8,128)(2,1)S(1)}, bf16[128,124]{1,0:T(8,128)(2,1)}, u32[]{:S(2)}) copy-start(bf16[128,124]{1,0:T(8,128)(2,1)} %reshape.298) | copy-start | bytes 95236 | tf_op jit(solution)/shard_map/while/body/eval_jaxpr/cond
  236.1 6.4 %collective-permute-start.3 = (bf16[128,256]{1,0:T(8,128)(2,1)}, bf16[128,256]{1,0:T(8,128)(2,1)S(1)}, u32[]{:S(2)}, u32[]{:S(2)}) collective-permute-start(bf16[128,256]{1,0:T(8,128)(2,1)} %fusion.84), channel_id=1, source_target_pairs={{4,0},{5,1},{6,2},{7,3},{12,8},{13,9},{14,10},{15,11},{20,16},{21,... | collective-permute-start | bytes 196616 | tf_op jit(solution)/shard_map/while/body/eval_jaxpr/ppermute | solution.py:30
  243.2 74.1 %all-reduce.2.cloned.1.call-start = ((), (), s32[]{:S(2)}) async-start(), calls=%async_computation.2 | async-start | bytes 524288 | tf_op jit(solution)/shard_map/while/body/eval_jaxpr/psum | solution.py:170
  244.2 3.3 copy-start.7
  280.9 4.2 %copy-start.4 = (bf16[1024,124]{1,0:T(8,128)(2,1)S(1)}, bf16[1024,124]{1,0:T(8,128)(2,1)}, u32[]{:S(2)}) copy-start(bf16[1024,124]{1,0:T(8,128)(2,1)} %get-tuple-element.580) | copy-start | bytes 761860 | tf_op jit(solution)/shard_map/while/body/eval_jaxpr/cond
  280.9 4.2 %copy-start.6 = (bf16[128,124]{1,0:T(8,128)(2,1)S(1)}, bf16[128,124]{1,0:T(8,128)(2,1)}, u32[]{:S(2)}) copy-start(bf16[128,124]{1,0:T(8,128)(2,1)} %reshape.298) | copy-start | bytes 95236 | tf_op jit(solution)/shard_map/while/body/eval_jaxpr/cond
  321.0 6.4 %collective-permute-start.3 = (bf16[128,256]{1,0:T(8,128)(2,1)}, bf16[128,256]{1,0:T(8,128)(2,1)S(1)}, u32[]{:S(2)}, u32[]{:S(2)}) collective-permute-start(bf16[128,256]{1,0:T(8,128)(2,1)} %fusion.84), channel_id=1, source_target_pairs={{4,0},{5,1},{6,2},{7,3},{12,8},{13,9},{14,10},{15,11},{20,16},{21,... | collective-permute-start | bytes 196616 | tf_op jit(solution)/shard_map/while/body/eval_jaxpr/ppermute | solution.py:30
  328.1 33.1 %reduce-scatter.2.cloned.1.call-start = ((), (), s32[]{:S(2)}) async-start(), calls=%async_computation.1 | async-start | bytes 1638400 | tf_op jit(solution)/shard_map/reduce_scatter | solution.py:196
  (7 other events, 11.4 us)
Sparse Core Ops, SparseCore 0:
  76.1 71.3 all-reduce.1
  201.3 31.0 all-reduce.1
  286.2 31.0 all-reduce.1
Sparse Core Ops, SparseCore 1:
  330.8 30.3 reduce-scatter.1
